TPU v7x, 256 devices: a whole 4x4x8 slice. The times are simulated.
256 devices in a mesh: ens: 16 (over z, y_hi), mp: 16 (over x, y_lo, core).
Axes of the slice: x: 4, y: 4 (y_hi: 2, y_lo: 2; y = y_hi * 2 + y_lo), z: 8, core: 2. Of those that a mesh axis runs over, the one named last changes fastest.
Arguments:
- tokens: bfloat16 [16, 8192, 1024], P('ens', 'mp'), may hold values from -6 to 6
- ln_gain: float32 [1024], replicated, may hold values from 0.5 to 1.5
- w_qkv: bfloat16 [1024, 3072], replicated, may hold values from -1 to 1
- w_out: bfloat16 [1024, 1024], replicated, may hold values from -0.75 to 0.75
- neighbours: int32 [4, 32768], P(None, 'mp'), may hold values from 0 to 8191, as said below
- edge_weights: float32 [4, 32768], P(None, 'mp'), may hold values from 0.2 to 1
- w_dec: bfloat16 [100, 1024], replicated, may hold values from -0.1875 to 0.1875
- truth: float32 [100, 32768], P(None, ('mp', 'ens')), may hold values from -6 to 6
Outputs:
- crps_score: float32 [100, 32768], P(None, ('mp', 'ens'))
Inputs may be any that keep to these rules, and one draw needn't show every extreme that they name: `neighbours`: the tokens of point g are among tokens g // 2048 * 512 to g // 2048 * 512 + 511 of its member.
All inputs are finite; a program needn't handle non-finite values.
Results may differ from a plain program's by a relative error of at most 0.0028.
The roundings to bfloat16 on the way count: a program that leaves them out, or rounds other values in their place, can miss the bound.
Values may be sent and summed in bfloat16 or wider, within the bound.
A program may use at most 128 MiB of HBM per device.

v0:
```python
import jax
import jax.numpy as jnp
from jax import lax
from jax.sharding import PartitionSpec as P

HEADS = 16
NEIGH = 4
HALF = 512


ALPHA = 0.95


def layer_norm(inputs, ln_gain):
    values = inputs.astype(jnp.float32)
    average = jnp.mean(values, axis=-1, keepdims=True)
    centred = values - average
    variance = jnp.mean(centred * centred, axis=-1, keepdims=True)
    return (centred * lax.rsqrt(variance + 1e-05) * ln_gain).astype(jnp.bfloat16)


def attend(queries, key_rows, value_rows, first_row, seq_tokens):
    count = queries.shape[1]
    head_dim = queries.shape[-1]
    scores = jnp.einsum(
        "mqhe,mkhe->mhqk", queries, key_rows, preferred_element_type=jnp.float32
    ) / jnp.sqrt(jnp.float32(head_dim))
    query_pos = first_row + jnp.arange(count, dtype=jnp.int32)
    key_pos = first_row - HALF + jnp.arange(count + 2 * HALF, dtype=jnp.int32)
    allowed = (
        (key_pos[None, :] >= 0)
        & (key_pos[None, :] < seq_tokens)
        & (jnp.abs(key_pos[None, :] - query_pos[:, None]) <= HALF)
    )
    scores = jnp.where(allowed[None, None], scores, -1e30)
    top = jnp.max(scores, axis=-1, keepdims=True)
    expo = jnp.exp(scores - top)
    weights = (expo / jnp.sum(expo, axis=-1, keepdims=True)).astype(jnp.bfloat16)
    context = jnp.einsum("mhqk,mkhe->mqhe", weights, value_rows, preferred_element_type=jnp.float32)
    return context.astype(jnp.bfloat16)


def shards(tokens, ln_gain, w_qkv, w_out, neighbours, edge_weights, w_dec, truth):
    members_here, tok_rows, model_width = tokens.shape
    lane_count = lax.axis_size("mp")
    lane_index = lax.axis_index("mp")
    seq_tokens = tok_rows * lane_count
    head_count = HEADS
    head_dim = model_width // head_count
    normed = layer_norm(tokens, ln_gain)
    projected = jnp.einsum("mtd,de->mte", normed, w_qkv, preferred_element_type=jnp.float32).astype(
        jnp.bfloat16
    )
    by_head = projected.reshape(members_here, tok_rows, 3, head_count, head_dim)
    regroup = lax.all_to_all(by_head, "mp", split_axis=3, concat_axis=1, tiled=True)
    local_heads = head_count // lane_count
    queries = regroup[:, :, 0]
    key_pad = jnp.pad(regroup[:, :, 1], ((0, 0), (HALF, HALF), (0, 0), (0, 0)))
    value_pad = jnp.pad(regroup[:, :, 2], ((0, 0), (HALF, HALF), (0, 0), (0, 0)))

    def block_attend(block_index):
        first_row = block_index * tok_rows
        query_block = lax.dynamic_slice_in_dim(queries, first_row, tok_rows, 1)
        key_block = lax.dynamic_slice_in_dim(key_pad, first_row, tok_rows + 2 * HALF, 1)
        value_block = lax.dynamic_slice_in_dim(value_pad, first_row, tok_rows + 2 * HALF, 1)
        return attend(query_block, key_block, value_block, first_row, seq_tokens)

    block_outs = lax.map(block_attend, jnp.arange(lane_count, dtype=jnp.int32))
    all_rows = jnp.moveaxis(block_outs, 0, 1).reshape(
        members_here, seq_tokens, local_heads, head_dim
    )
    context = lax.all_to_all(all_rows, "mp", split_axis=1, concat_axis=2, tiled=True)
    context = context.reshape(members_here, tok_rows, model_width)
    proj_out = jnp.einsum("mtd,de->mte", context, w_out, preferred_element_type=jnp.float32)
    processed = (tokens.astype(jnp.float32) + proj_out).astype(jnp.bfloat16)
    local_index = neighbours - lane_index * tok_rows
    hidden = jnp.zeros((members_here, neighbours.shape[1], model_width), jnp.float32)
    for slot_index in range(NEIGH):
        picked = jnp.take(processed, local_index[slot_index], axis=1)
        hidden = hidden + edge_weights[slot_index][None, :, None] * picked.astype(jnp.float32)
    decoded = jnp.einsum(
        "vd,mgd->mvg", w_dec, hidden.astype(jnp.bfloat16), preferred_element_type=jnp.float32
    ).astype(jnp.bfloat16)
    gathered = lax.all_to_all(decoded, "ens", split_axis=2, concat_axis=0, tiled=True).astype(
        jnp.float32
    )
    member_total = gathered.shape[0]
    skill_term = jnp.mean(jnp.abs(gathered - truth[None]), axis=0)
    spread = jnp.sum(jnp.abs(gathered[:, None] - gathered[None, :]), axis=(0, 1))
    coeff = ALPHA / (2.0 * member_total * (member_total - 1)) + (1.0 - ALPHA) / (
        2.0 * member_total * member_total
    )
    return skill_term - coeff * spread


def solution(mesh):
    in_specs = (
        P("ens", "mp", None),
        P(),
        P(),
        P(),
        P(None, "mp"),
        P(None, "mp"),
        P(),
        P(None, ("mp", "ens")),
    )
    out_specs = P(None, ("mp", "ens"))
    return jax.shard_map(shards, mesh=mesh, in_specs=in_specs, out_specs=out_specs, check_vma=False)
```

profile of v0, /device:TPU:8, one launch (start us, length us, event | category | flops | bytes accessed | tf_op | source)
XLA Modules:
  0.0 371.9 jit_solution(4626940275149164872)
XLA Ops:
  3.2 8.3 %convolution_convert_fusion = bf16[512,3072]{1,0:T(8,128)(2,1)} fusion(bf16[1024,3072]{1,0:T(8,128)(2,1)} %param.14, bf16[1,512,1024]{2,1,0:T(8,128)(2,1)} %param.12, f32[1024]{0:T(1024)} %param.13, f32[512]{0:T(512)S(1)} %add_rsqrt_fusion, f32[512]{0:T(512)S(1)} %broadcast_multiply_fusion), kind=kOutput, calls=%fused_computation.28 | convolution fusion | flops 3225419776 | bytes 10493952 | tf_op jit(solution)/shard_map/mtd,de->mte/dot_general | solution.py:51
  11.5 4.7 %copy.45 = bf16[512,3072]{0,1:T(8,128)(2,1)} copy(bf16[512,3072]{1,0:T(8,128)(2,1)} %convolution_convert_fusion) | data formatting | bytes 6291456 | tf_op jit(solution)/shard_map/convert_element_type | solution.py:51
  16.2 3.9 %copy.46 = bf16[1,512,3,16,64]{1,4,2,0,3:T(8,128)(2,1)} copy(bf16[1,512,3,16,64]{1,4,3,2,0:T(8,128)(2,1)} %bitcast.144) | data formatting | bytes 6291456 | tf_op jit(solution)/shard_map/reshape | solution.py:54
  20.2 6.5 %all-to-all-start = ((bf16[1,512,3,16,64]{1,4,2,0,3:T(8,128)(2,1)}), bf16[1,512,3,16,64]{1,4,2,0,3:T(8,128)(2,1)}, u32[]{:S(2)}, u32[]{:S(2)}) async-start(bf16[1,512,3,16,64]{1,4,2,0,3:T(8,128)(2,1)} %copy.46), calls=%async_computation | async-start | bytes 6291456 | tf_op jit(solution)/shard_map/all_to_all | solution.py:55
  26.8 42.5 %all-to-all-done = bf16[1,512,3,16,64]{1,4,2,0,3:T(8,128)(2,1)} async-done(((bf16[1,512,3,16,64]{1,4,2,0,3:T(8,128)(2,1)}), bf16[1,512,3,16,64]{1,4,2,0,3:T(8,128)(2,1)}, u32[]{:S(2)}, u32[]{:S(2)}) %all-to-all-start) | async-done | bytes 3145760 | tf_op jit(solution)/shard_map/all_to_all | solution.py:55
  74.2 92.6 %while.12 = (s32[]{:T(128)}, bf16[16,1,512,1,64]{2,4,3,1,0:T(8,128)(2,1)}, s32[16]{0:T(128)S(1)}, bf16[1,9216,1,64]{1,3,2,0:T(8,128)(2,1)S(1)}, bf16[1,8192,1,64...) while((s32[]{:T(128)}, ...), condition=%wide.region_5.6_spmd, body=%wide.region_2.5_spmd.sunk | while | flops 210803712 | bytes 9991916 | solution.py:68
  87.1 2.4 fusion.54
  98.7 2.4 fusion.54
  104.5 2.4 fusion.54
  116.0 2.4 fusion.54
  127.6 2.4 fusion.54
  133.4 2.4 fusion.54
  139.2 2.4 fusion.54
  145.0 2.4 fusion.54
  150.7 2.4 fusion.54
  156.5 2.4 fusion.54
  166.7 2.8 copy.55
  169.5 12.5 %reshape.226 = bf16[1,8192,1,64]{3,2,0,1:T(2,128)(2,1)} reshape(bf16[16,1,512,1,64]{4,2,0,3,1:T(8,128)(2,1)} %copy.55) | data formatting | bytes 2097152 | tf_op jit(solution)/shard_map/reshape;transpose | solution.py:69
  182.5 46.5 %reduce.12 = bf16[8192,64]{1,0:T(8,128)(2,1)} reduce(bf16[8192,1,1,64]{3,2,1,0:T(2,128)(2,1)} %bitcast.139, bf16[]{:T(256)} %broadcast.155), dimensions={1,2}, to_apply=%bitcast.116.reduce_sub_computation | reduce | bytes 2097154
  229.0 4.7 %reshape.227 = bf16[16,2,16384]{2,1,0:T(2,128)(2,1)} reshape(bf16[8192,64]{1,0:T(8,128)(2,1)} %reduce.12) | data formatting | bytes 2097152
  233.7 4.4 %all-to-all-start.1 = ((bf16[16,2,16384]{2,1,0:T(2,128)(2,1)}), bf16[16,2,16384]{2,1,0:T(2,128)(2,1)S(1)}, u32[]{:S(2)}, u32[]{:S(2)}) async-start(bf16[16,2,16384]{2,1,0:T(2,128)(2,1)} %reshape.227), calls=%async_computation.1 | async-start | bytes 2097152 | tf_op jit(solution)/shard_map/all_to_all | solution.py:72
  238.1 14.8 %all-to-all-done.1 = bf16[16,2,16384]{2,1,0:T(2,128)(2,1)S(1)} async-done(((bf16[16,2,16384]{2,1,0:T(2,128)(2,1)}), bf16[16,2,16384]{2,1,0:T(2,128)(2,1)S(1)}, u32[]{:S(2)}, u32[]{:S(2)}) %all-to-all-start.1) | async-done | bytes 1048608 | tf_op jit(solution)/shard_map/all_to_all | solution.py:72
  252.9 7.0 %reshape.228 = bf16[8192,1,1,64]{3,2,1,0:T(2,128)(2,1)} reshape(bf16[16,2,16384]{2,1,0:T(2,128)(2,1)S(1)} %all-to-all-done.1) | data formatting | bytes 2097152
  259.9 8.2 %copy.50 = bf16[1,8192,1,64]{1,3,2,0:T(8,128)(2,1)S(1)} copy(bf16[1,8192,1,64]{3,2,0,1:T(2,128)(2,1)} %bitcast.138) | data formatting | bytes 2097152 | tf_op jit(solution)/shard_map/all_to_all | solution.py:72
  270.6 9.6 %gather_fusion = bf16[2048,1024]{1,0:T(8,128)(2,1)} fusion(bf16[512,1024]{1,0:T(8,128)(2,1)S(1)} %fusion.31, s32[2048]{0:T(1024)S(1)} %fusion.37), kind=kCustom, calls=%fused_computation.clone | custom fusion | bytes 8396800 | tf_op jit(solution)/shard_map/jit(_take)/gather | solution.py:79
  280.3 9.7 %gather_fusion.1 = bf16[2048,1024]{1,0:T(8,128)(2,1)} fusion(bf16[512,1024]{1,0:T(8,128)(2,1)S(1)} %fusion.31, s32[2048]{0:T(1024)S(1)} %fusion.38), kind=kCustom, calls=%fused_computation.1.clone | custom fusion | bytes 8396800 | tf_op jit(solution)/shard_map/jit(_take)/gather | solution.py:79
  289.9 9.7 %gather_fusion.2 = bf16[2048,1024]{1,0:T(8,128)(2,1)} fusion(bf16[512,1024]{1,0:T(8,128)(2,1)S(1)} %fusion.31, s32[2048]{0:T(1024)S(1)} %fusion.39), kind=kCustom, calls=%fused_computation.2.clone | custom fusion | bytes 8396800 | tf_op jit(solution)/shard_map/jit(_take)/gather | solution.py:79
  299.6 9.7 %gather_fusion.3 = bf16[2048,1024]{1,0:T(8,128)(2,1)} fusion(bf16[512,1024]{1,0:T(8,128)(2,1)S(1)} %fusion.31, s32[2048]{0:T(1024)S(1)} %fusion.40), kind=kCustom, calls=%fused_computation.3.clone | custom fusion | bytes 8396800 | tf_op jit(solution)/shard_map/jit(_take)/gather | solution.py:79
  309.3 9.7 %fusion.23 = bf16[1,100,2048]{2,1,0:T(8,128)(2,1)S(1)} fusion(bf16[100,1024]{1,0:T(8,128)(2,1)S(1)} %copy-done.6, bf16[2048,1024]{1,0:T(8,128)(2,1)} %gather_fusion.3, bf16[2048,1024]{1,0:T(8,128)(2,1)} %gather_fusion.2, bf16[2048,1024]{1,0:T(8,128)(2,1)} %gather_fusion.1, bf16[2048,1024]{1,0:T(8,128)(2,1)} %gather_fusion, f32[2048]{0:T(1024)S(1)} %bitcast.160, ...), kind=kOutput, calls=%fused_computation.41 | convolution fusion | flops 453189632 | bytes 17432576 | tf_op jit(solution)/shard_map/vd,mgd->mvg/dot_general | solution.py:81
  319.7 11.8 %reduce.13 = bf16[2048,100]{1,0:T(8,128)(2,1)S(1)} reduce(bf16[2048,1,100]{2,1,0:T(2,128)(2,1)S(1)} %bitcast.147, bf16[]{:T(256)} %broadcast.155), dimensions={1}, to_apply=%bitcast.118.reduce_sub_computation | reduce | bytes 819202
  333.2 27.9 %all_to_all.42 = bf16[16,2,6400]{2,1,0:T(2,128)(2,1)S(1)} all-to-all(bf16[16,2,6400]{2,1,0:T(2,128)(2,1)S(1)} %reshape.229), channel_id=1, replica_groups=mesh['ens'=16,'mp'=16] {'ens'}, dimensions={0} | all-to-all | bytes 819200 | tf_op jit(solution)/shard_map/all_to_all | solution.py:84
  363.3 3.8 %copy.53 = bf16[1,100,2048]{2,0,1:T(2,128)(2,1)} copy(bf16[1,100,2048]{1,0,2:T(2,128)(2,1)S(1)} %bitcast.146) | data formatting | bytes 819200 | tf_op jit(solution)/shard_map/all_to_all | solution.py:84
  (147 shorter events, 77.9 us)
Async XLA Ops:
  0.0 269.0 %copy-start = (bf16[1024,1024]{1,0:T(8,128)(2,1)S(1)}, bf16[1024,1024]{1,0:T(8,128)(2,1)}, u32[]{:S(2)}) copy-start(bf16[1024,1024]{1,0:T(8,128)(2,1)} %param.15) | copy-start | bytes 6291460
  20.2 6.5 %copy-start.4 = (s32[4,2048]{1,0:T(4,128)S(1)}, s32[4,2048]{1,0:T(4,128)}, u32[]{:S(2)}) copy-start(s32[4,2048]{1,0:T(4,128)} %param.16) | copy-start | bytes 98308
  20.2 49.2 %all-to-all-start = ((bf16[1,512,3,16,64]{1,4,2,0,3:T(8,128)(2,1)}), bf16[1,512,3,16,64]{1,4,2,0,3:T(8,128)(2,1)}, u32[]{:S(2)}, u32[]{:S(2)}) async-start(bf16[1,512,3,16,64]{1,4,2,0,3:T(8,128)(2,1)} %copy.46), calls=%async_computation | async-start | bytes 6291456 | tf_op jit(solution)/shard_map/all_to_all | solution.py:55
  229.0 9.1 %copy-start.5 = (f32[4,2048]{1,0:T(4,128)S(1)}, f32[4,2048]{1,0:T(4,128)}, u32[]{:S(2)}) copy-start(f32[4,2048]{1,0:T(4,128)} %param.17) | copy-start | bytes 98308
  233.7 19.2 %all-to-all-start.1 = ((bf16[16,2,16384]{2,1,0:T(2,128)(2,1)}), bf16[16,2,16384]{2,1,0:T(2,128)(2,1)S(1)}, u32[]{:S(2)}, u32[]{:S(2)}) async-start(bf16[16,2,16384]{2,1,0:T(2,128)(2,1)} %reshape.227), calls=%async_computation.1 | async-start | bytes 2097152 | tf_op jit(solution)/shard_map/all_to_all | solution.py:72
  268.1 1.2 copy-start.2
  299.6 9.7 %copy-start.6 = (bf16[100,1024]{1,0:T(8,128)(2,1)S(1)}, bf16[100,1024]{1,0:T(8,128)(2,1)}, u32[]{:S(2)}) copy-start(bf16[100,1024]{1,0:T(8,128)(2,1)} %param.18) | copy-start | bytes 614404
  363.3 7.7 %copy-start.3 = (f32[100,128]{1,0:T(8,128)S(1)}, f32[100,128]{1,0:T(8,128)}, u32[]{:S(2)}) copy-start(f32[100,128]{1,0:T(8,128)} %param.19) | copy-start | bytes 153604
  363.3 8.6 %copy-start.1 = (bf16[1024,1024]{1,0:T(8,128)(2,1)S(1)}, bf16[1024,1024]{1,0:T(8,128)(2,1)}, u32[]{:S(2)}) copy-start(bf16[1024,1024]{1,0:T(8,128)(2,1)} %param.15) | copy-start | bytes 6291460
where the time goes:
time: 374 us; the launch traced here: 372 us
  local copies, waits for them, and re-layouts  108 us (29%)
  matrix products  80.5 us (22%)
  other arithmetic  75.6 us (20%)
  waiting for transfers between devices  57.3 us (15%)
  blocking collectives  27.9 us (7%)
  loops' own time  11.5 us (3%)
  starting transfers between devices  10.9 us (3%)
    unnamed x2, other arithmetic  58.3 us
    all_to_all x1, waiting for transfers between devices, shards(): lax.all_to_all(by_head, 'mp', split_axis=3, concat_axis=1, tiled=True)  42.5 us
    gather x4, local copies, waits for them, and re-layouts, shards(): picked = jnp.take(processed, local_index[slot_index], axis=1)  38.6 us
    dot_general x16, matrix products, attend(): jnp.einsum('mqhe,mkhe->mhqk', queries, key_rows, preferred_element_type=j...  38 us
    all_to_all x1, blocking collectives, shards(): lax.all_to_all(decoded, 'ens', split_axis=2, concat_axis=0, tiled=True)  27.9 us
    dot_general x16, matrix products, attend(): jnp.einsum('mhqk,mkhe->mqhe', weights, value_rows, preferred_element_type...  23.2 us
    unnamed x20, local copies, waits for them, and re-layouts  16.7 us
    another operation x2, local copies, waits for them, and re-layouts, shards(): jnp.moveaxis(block_outs, 0, 1)  15.3 us
  transfers between devices with their start and end apart: 2, of which 2 were waited for; matrix products, arithmetic and copies ran while one was open for 0% of the time, Pallas kernels for 0%

commit v1 on v0

v1 whole, which is shorter than its diff:
```python
import functools

import jax
import jax.numpy as jnp
from jax import lax
from jax.experimental import pallas as pl
from jax.experimental.pallas import tpu as pltpu
from jax.sharding import PartitionSpec as P

HEADS = 16
NEIGH = 4
HALF = 512
ALPHA = 0.95
F32 = jnp.float32
BF16 = jnp.bfloat16
MESH = pl.DeviceIdType.MESH


def dot(a, b):
    return lax.dot_general(a, b, (((1,), (0,)), ((), ())), preferred_element_type=F32)


def dot_t(a, b):
    return lax.dot_general(a, b, (((1,), (1,)), ((), ())), preferred_element_type=F32)


def split(x):
    hi = x.astype(BF16)
    lo = (x - hi.astype(F32)).astype(BF16)
    return hi, lo


def norm_rows(src, dst, gain_ref, rows):
    block = 64

    def step(i, carry):
        sl = pl.ds(pl.multiple_of(i * block, block), block)
        x = src[sl, :].astype(F32)
        mean = jnp.mean(x, axis=-1, keepdims=True)
        c = x - mean
        var = jnp.mean(c * c, axis=-1, keepdims=True)
        dst[sl, :] = (c * lax.rsqrt(var + 1e-05) * gain_ref[...]).astype(BF16)
        return carry

    lax.fori_loop(0, rows // block, step, 0)


def kernel(
    n_ens, n_mp, rows, grid_rows, n_vars,
    tok_hbm, gain_ref, wqkv_hbm, wout_hbm, nbr_ref, ew_ref, wdec_ref, truth_ref,
    out_ref,
    tok, halo, wqkv, wout, normed, qkv, kv, bias, o_acc, m_acc, l_acc, ctx, w2, sel_hi, sel_lo,
    d_hl, dec, got,
    in_sem, send_sem, recv_sem, a2a_send, a2a_recv,
):
    width = tok.shape[1]
    pairs = width // 128
    me = lax.axis_index("mp")
    ens = lax.axis_index("ens")
    core = lax.rem(me, 2)
    partner = me + 1 - 2 * core
    other = me - 1 + 2 * core
    has_other = jnp.logical_and(other >= 0, other < n_mp)

    loads = [
        pltpu.make_async_copy(tok_hbm.at[0], tok, in_sem.at[0]),
        pltpu.make_async_copy(wqkv_hbm, wqkv, in_sem.at[1]),
        pltpu.make_async_copy(wout_hbm, wout, in_sem.at[2]),
    ]
    for load in loads:
        load.start()

    barrier = pltpu.get_barrier_semaphore()
    pl.semaphore_signal(barrier, inc=1, device_id={"mp": partner}, device_id_type=MESH)

    around = lax.rem(other + n_mp, n_mp)
    pl.semaphore_signal(barrier, inc=1, device_id={"mp": around}, device_id_type=MESH)
    for step in range(1, n_ens):
        peer = lax.rem(ens + step, n_ens)
        pl.semaphore_signal(barrier, inc=1, device_id={"ens": peer}, device_id_type=MESH)

    loads[0].wait()
    norm_rows(tok, normed, gain_ref, rows)

    pl.semaphore_wait(barrier, n_ens + 1)

    def send_to(slot, target):
        return pltpu.make_async_remote_copy(
            src_ref=tok_hbm.at[0],
            dst_ref=halo.at[slot],
            send_sem=send_sem.at[slot],
            recv_sem=recv_sem.at[slot],
            device_id={"mp": target},
            device_id_type=MESH,
        )

    send_to(0, partner).start()

    @pl.when(has_other)
    def _():
        send_to(1, other).start()

    loads[1].wait()
    chunk = 512
    n_q = width // chunk

    def project_q(i, carry):
        cols = pl.ds(pl.multiple_of(i * chunk, chunk), chunk)
        qkv[:, cols] = dot(normed[...], wqkv[:, cols]).astype(BF16) * 0.125
        return carry

    def project_kv(i, carry):
        cols = pl.ds(pl.multiple_of(width + i * chunk, chunk), chunk)
        qkv[:, cols] = dot(normed[...], wqkv[:, cols]).astype(BF16)
        return carry

    lax.fori_loop(0, n_q, project_q, 0)
    lax.fori_loop(0, 2 * n_q, project_kv, 0)

    ones = jnp.ones((rows, 128), BF16)
    half_rows = rows // 2
    ones_h = jnp.ones((half_rows, 128), BF16)

    def first_half(n):
        return lax.broadcasted_iota(jnp.int32, (n, 128), 1) < 64

    def own_pair(hp, carry):
        cols = pl.ds(pl.multiple_of(hp * 128, 128), 128)
        kcols = pl.ds(pl.multiple_of(width + hp * 128, 128), 128)
        vcols = pl.ds(pl.multiple_of(2 * width + hp * 128, 128), 128)
        k = qkv[:, kcols]
        vx = jnp.concatenate([qkv[:, vcols], ones], axis=1)
        lanes = first_half(half_rows)
        for t in range(2):
            rs = pl.ds(t * half_rows, half_rows)
            q = qkv[rs, cols]
            zero = jnp.zeros_like(q)
            parts = []
            for part in range(2):
                qm = jnp.where(lanes, q, zero) if part == 0 else jnp.where(lanes, zero, q)
                s = dot_t(qm, k)
                m = jnp.max(s, axis=1, keepdims=True)
                p = jnp.exp(s - m).astype(BF16)
                parts.append((dot(p, vx), m))
            (o0, m0), (o1, m1) = parts
            o_acc[rs, cols] = jnp.where(lanes, o0[:, :128], o1[:, :128])
            l_acc[rs, cols] = jnp.where(lanes, o0[:, 128:], o1[:, 128:])
            m_acc[rs, cols] = jnp.where(lanes, m0, m1)
        return carry

    lax.fori_loop(0, pairs, own_pair, 0)

    loads[2].wait()
    w2_hi, w2_lo = split(dot_t(wdec_ref[...], wout[...]))
    w2[0] = w2_hi
    w2[1] = w2_lo
    base = me * rows
    gchunk = 256

    def build(i, carry):
        cols = pl.ds(pl.multiple_of(i * gchunk, gchunk), gchunk)
        t = lax.broadcasted_iota(jnp.int32, (rows, gchunk), 0)
        acc = jnp.zeros((rows, gchunk), F32)
        for k in range(NEIGH):
            idx = nbr_ref[k : k + 1, cols] - base
            w = ew_ref[k : k + 1, cols]
            acc = acc + jnp.where(t == idx, w, 0.0)
        hi, lo = split(acc)
        sel_hi[:, cols] = hi
        sel_lo[:, cols] = lo
        return carry

    lax.fori_loop(0, grid_rows // gchunk, build, 0)

    def segment(slot, left):
        norm_rows(halo.at[slot], normed, gain_ref, rows)

        def project(i, carry):
            src = pl.ds(pl.multiple_of(width + i * chunk, chunk), chunk)
            dst = pl.ds(pl.multiple_of(i * chunk, chunk), chunk)
            kv[:, dst] = dot(normed[...], wqkv[:, src]).astype(BF16)
            return carry

        lax.fori_loop(0, 2 * n_q, project, 0)
        sign = 2 * left - 1
        ii = lax.broadcasted_iota(jnp.int32, (half_rows, half_rows), 0)
        jj = lax.broadcasted_iota(jnp.int32, (half_rows, half_rows), 1)
        bias[...] = jnp.where((jj - ii) * sign >= 0, 0.0, -1e30)
        near = pl.multiple_of((1 - left) * half_rows, half_rows)
        far = pl.multiple_of(left * half_rows, half_rows)

        def pair(hp, carry):
            cols = pl.ds(pl.multiple_of(hp * 128, 128), 128)
            vcols = pl.ds(pl.multiple_of(width + hp * 128, 128), 128)
            lanes = first_half(half_rows)
            k_n = kv[pl.ds(near, half_rows), cols]
            k_f = kv[pl.ds(far, half_rows), cols]
            v_n = jnp.concatenate([kv[pl.ds(near, half_rows), vcols], ones_h], axis=1)
            v_f = jnp.concatenate([kv[pl.ds(far, half_rows), vcols], ones_h], axis=1)
            for wide in (True, False):
                rs = pl.ds(near if wide else far, half_rows)
                q = qkv[rs, cols]
                zero = jnp.zeros_like(q)
                parts = []
                for part in range(2):
                    qm = jnp.where(lanes, q, zero) if part == 0 else jnp.where(lanes, zero, q)
                    if wide:
                        s_n = dot_t(qm, k_n) + bias[...]
                        s_f = dot_t(qm, k_f)
                        m = jnp.maximum(
                            jnp.max(s_n, axis=1, keepdims=True), jnp.max(s_f, axis=1, keepdims=True)
                        )
                        o = dot(jnp.exp(s_n - m).astype(BF16), v_n)
                        o = o + dot(jnp.exp(s_f - m).astype(BF16), v_f)
                    else:
                        s_f = dot_t(qm, k_f) + bias[...]
                        m = jnp.max(s_f, axis=1, keepdims=True)
                        o = dot(jnp.exp(s_f - m).astype(BF16), v_f)
                    parts.append((o, m))
                (o0, m0), (o1, m1) = parts
                o = jnp.where(lanes, o0[:, :128], o1[:, :128])
                l = jnp.where(lanes, o0[:, 128:], o1[:, 128:])
                m = jnp.where(lanes, m0, m1)
                m_old = m_acc[rs, cols]
                m_new = jnp.maximum(m_old, m)
                a = jnp.exp(m_old - m_new)
                b = jnp.exp(m - m_new)
                o_acc[rs, cols] = o_acc[rs, cols] * a + o * b
                l_acc[rs, cols] = l_acc[rs, cols] * a + l * b
                m_acc[rs, cols] = m_new
            return carry

        lax.fori_loop(0, pairs, pair, 0)

    send_to(0, partner).wait()
    segment(0, core)

    @pl.when(has_other)
    def _():
        send_to(1, other).wait()
        segment(1, 1 - core)

    def finish(i, carry):
        sl = pl.ds(pl.multiple_of(i * 32, 32), 32)
        ctx[sl, :] = (o_acc[sl, :] / l_acc[sl, :]).astype(BF16)
        return carry

    lax.fori_loop(0, rows // 32, finish, 0)

    d = dot_t(w2[0], ctx[...]) + dot_t(w2[1], ctx[...]) + dot_t(wdec_ref[...], tok[...])
    d_hi, d_lo = split(d)
    d_hl[0] = d_hi
    d_hl[1] = d_lo
    points = grid_rows // n_ens
    per = gchunk // points

    def decode(i, carry):
        cols = pl.ds(pl.multiple_of(i * gchunk, gchunk), gchunk)
        hi = sel_hi[:, cols]
        r = dot(d_hl[0], hi) + dot(d_hl[1], hi) + dot(d_hl[0], sel_lo[:, cols])
        r = r.astype(BF16)
        for j in range(per):
            dec[i * per + j] = r[:, j * points : (j + 1) * points]
        return carry

    lax.fori_loop(0, grid_rows // gchunk, decode, 0)

    def to_peer(step):
        peer = lax.rem(ens + step, n_ens)
        return pltpu.make_async_remote_copy(
            src_ref=dec.at[peer],
            dst_ref=got.at[step],
            send_sem=a2a_send.at[step],
            recv_sem=a2a_recv.at[step],
            device_id={"ens": peer},
            device_id_type=MESH,
        )

    for step in range(1, n_ens):
        to_peer(step).start()
    got[0] = dec[ens]
    for step in range(1, n_ens):
        to_peer(step).wait()

    coeff = ALPHA / (2.0 * n_ens * (n_ens - 1)) + (1.0 - ALPHA) / (2.0 * n_ens * n_ens)

    def score(sl):
        truth = truth_ref[sl, :]
        members = [got[j, sl, :].astype(F32) for j in range(n_ens)]
        skill = jnp.zeros_like(truth)
        spread = jnp.zeros_like(truth)
        for j in range(n_ens):
            skill = skill + jnp.abs(members[j] - truth)
            for k in range(j + 1, n_ens):
                spread = spread + jnp.abs(members[j] - members[k])
        out_ref[sl, :] = skill * (1.0 / n_ens) - (2.0 * coeff) * spread

    def score_block(i, carry):
        score(pl.ds(pl.multiple_of(i * 16, 16), 16))
        return carry

    whole = n_vars // 16
    lax.fori_loop(0, whole, score_block, 0)
    if n_vars % 16:
        score(slice(whole * 16, n_vars))


def solution(mesh):
    n_ens, n_mp = mesh.shape["ens"], mesh.shape["mp"]

    def shards(tokens, ln_gain, w_qkv, w_out, neighbours, edge_weights, w_dec, truth):
        rows, width = tokens.shape[1:]
        grid_rows = neighbours.shape[1]
        n_vars, points = truth.shape
        hbm = pl.BlockSpec(memory_space=pl.ANY)
        vmem = pl.BlockSpec(memory_space=pltpu.VMEM)
        return pl.pallas_call(
            functools.partial(kernel, n_ens, n_mp, rows, grid_rows, n_vars),
            out_shape=jax.ShapeDtypeStruct((n_vars, points), F32),
            in_specs=[hbm, vmem, hbm, hbm, vmem, vmem, vmem, vmem],
            out_specs=vmem,
            scratch_shapes=[
                pltpu.VMEM((rows, width), BF16),
                pltpu.VMEM((2, rows, width), BF16),
                pltpu.VMEM((width, 3 * width), BF16),
                pltpu.VMEM((width, width), BF16),
                pltpu.VMEM((rows, width), BF16),
                pltpu.VMEM((rows, 3 * width), BF16),
                pltpu.VMEM((rows, 2 * width), BF16),
                pltpu.VMEM((rows // 2, rows // 2), F32),
                pltpu.VMEM((rows, width), F32),
                pltpu.VMEM((rows, width), F32),
                pltpu.VMEM((rows, width), F32),
                pltpu.VMEM((rows, width), BF16),
                pltpu.VMEM((2, n_vars, width), BF16),
                pltpu.VMEM((rows, grid_rows), BF16),
                pltpu.VMEM((rows, grid_rows), BF16),
                pltpu.VMEM((2, n_vars, rows), BF16),
                pltpu.VMEM((n_ens, n_vars, points), BF16),
                pltpu.VMEM((n_ens, n_vars, points), BF16),
                pltpu.SemaphoreType.DMA((3,)),
                pltpu.SemaphoreType.DMA((2,)),
                pltpu.SemaphoreType.DMA((2,)),
                pltpu.SemaphoreType.DMA((n_ens,)),
                pltpu.SemaphoreType.DMA((n_ens,)),
            ],
            compiler_params=pltpu.CompilerParams(
                collective_id=0, has_side_effects=True, vmem_limit_bytes=62 * 1024 * 1024
            ),
        )(tokens, ln_gain.reshape(1, width), w_qkv, w_out, neighbours, edge_weights, w_dec, truth)

    in_specs = (
        P("ens", "mp", None),
        P(),
        P(),
        P(),
        P(None, "mp"),
        P(None, "mp"),
        P(),
        P(None, ("mp", "ens")),
    )
    out_specs = P(None, ("mp", "ens"))
    return jax.shard_map(shards, mesh=mesh, in_specs=in_specs, out_specs=out_specs, check_vma=False)
```

time: 374 us -> 69.8 us (0.19)
  local copies, waits for them, and re-layouts: 108 us -> 1.43 us
  matrix products: 80.5 us -> 0 us
  other arithmetic: 75.6 us -> 0 us
  Pallas kernels: 0 us -> 67.1 us
  waiting for transfers between devices: 57.3 us -> 0 us
  blocking collectives: 27.9 us -> 0 us
  loops' own time: 11.5 us -> 0 us
  starting transfers between devices: 10.9 us -> 0 us
    dot_general x35 -> x0, matrix products: 80.5 us -> none  [the longest x16 38 us: attend(): jnp.einsum('mqhe,mkhe->mhqk', queries, key_rows, preferred_element_type=j...]
    pallas_call x0 -> x1, Pallas kernels: none -> 67.1 us  [shards(): pl.pallas_call(functools.partial(kernel, n_ens, n_mp, rows, grid_rows, n_...]
    unnamed x2 -> x0, other arithmetic: 58.3 us -> none
    all_to_all x2 -> x0, waiting for transfers between devices: 57.3 us -> none  [the longest x1 42.5 us: shards(): lax.all_to_all(by_head, 'mp', split_axis=3, concat_axis=1, tiled=True)]
    gather x4 -> x0, local copies, waits for them, and re-layouts: 38.6 us -> none  [shards(): picked = jnp.take(processed, local_index[slot_index], axis=1)]
    all_to_all x1 -> x0, blocking collectives: 27.9 us -> none  [shards(): lax.all_to_all(decoded, 'ens', split_axis=2, concat_axis=0, tiled=True)]
    unnamed x20 -> x1, local copies, waits for them, and re-layouts: 16.7 us -> 1.43 us
    another operation x2 -> x0, local copies, waits for them, and re-layouts: 15.3 us -> none  [shards(): jnp.moveaxis(block_outs, 0, 1)]
  transfers between devices with their start and end apart: 2 -> 0, of which waited for: 2 -> 0; matrix products, arithmetic and copies ran while one was open for 0% -> 0% of each run, Pallas kernels for 0% -> 0%
where the time goes in v1:
time: 69.8 us; the launch traced here: 68.5 us
  Pallas kernels  67.1 us (96%)
  local copies, waits for them, and re-layouts  1.43 us (2%)
    pallas_call x1, Pallas kernels, shards(): pl.pallas_call(functools.partial(kernel, n_ens, n_mp, rows, grid_rows, n_...  67.1 us
    unnamed x1, local copies, waits for them, and re-layouts  1.43 us

profile of v1, /device:TPU:8, one launch (start us, length us, event | category | flops | bytes accessed | tf_op | source)
XLA Modules:
  0.0 68.5 jit_solution(685241546040137223)
XLA Ops:
  0.0 67.1 %shard_map.82 = f32[100,128]{1,0:T(8,128)} custom-call(bf16[1,512,1024]{2,1,0:T(8,128)(2,1)} %tok_hbm.1, f32[1,1024]{1,0:T(1,128)} %bitcast.1, bf16[1024,3072]{1,0:T(8,128)(2,1)} %wqkv_hbm.1, bf16[1024,1024]{1,0:T(8,128)(2,1)} %wout_hbm.1, s32[4,2048]{1,0:T(4,128)} %nbr_ref.1, f32[4,2048]{1,0:T(4,128)} %ew_ref.1, bf16[100,1024]{1,0:T(8,128)(2,1)} %wdec_ref.1, ...), custom_call_target="tpu_custom_call" | custom-call | tf_op jit(solution)/shard_map/pallas_call | solution.py:317
  67.1 1.4 %copy.10 = f32[100,128]{1,0:T(8,128)} copy(f32[100,128]{1,0:T(8,128)} %shard_map.82) | data formatting | bytes 102400
